TPU v7x, 32 devices: a whole 2x2x4 slice. The times are simulated.
32 devices in a mesh: groups: 2 (over y), lib: 4 (over z), tmpl: 2 (over x), sub: 2 (over core).
Axes of the slice: x: 2, y: 2, z: 4, core: 2. Of those that a mesh axis runs over, the one named last changes fastest.
Arguments:
- coords: float32 [512, 3, 128], P(('groups', 'lib', 'tmpl')), parts along dimension 0, may hold values from -5 to 5
- atom_type: int32 [512, 128], P(('groups', 'lib', 'tmpl')), parts along dimension 0, may hold values from 0 to 15
- channel: int32 [512, 128], P(('groups', 'lib', 'tmpl')), parts along dimension 0, may hold values from 0 to 2
- charge: float32 [512, 128], P(('groups', 'lib', 'tmpl')), parts along dimension 0, may hold values from -3 to 3
- pair_owner: int32 [512, 4], P(('groups', 'lib', 'tmpl')), parts along dimension 0, may hold values from 0 to 7, all different within a row; in each aligned block of 32 rows (0 to 31, 32 to 63, ...) at most 32 rows name the same one
- pair_slot: int32 [512, 4], P(('groups', 'lib', 'tmpl')), parts along dimension 0, may hold values from 0 to 511
- type_table: float32 [16, 2], replicated, may hold values from 0.3 to 3
- widths: float32 [5], replicated, may hold values from 0.3 to 1.2
- tmpl_points: float32 [4096, 3, 256], P(('lib', 'tmpl'), None, 'sub'), may hold values from -5 to 5
- tmpl_weights: bfloat16 [4096, 5, 256], P(('lib', 'tmpl'), None, 'sub'), may hold values from -3 to 3
Outputs:
- scores: float32 [512, 4], P(('groups', 'lib', 'tmpl')), parts along dimension 0
- pose_grad: float32 [512, 12], P(('groups', 'lib', 'tmpl')), parts along dimension 0
- weight_grad: float32 [8192, 5, 256], P(('groups', 'lib', 'tmpl'), None, 'sub'), parts along dimension 0
There are 2 independent parts, one for each index of `groups`. A program takes and returns all parts, laid end to end along the dimension named above; an argument that names none is the same for every part. Nothing has to cross between parts.
Inputs may be any that keep to these rules, and one draw needn't show every extreme that they name: `pair_owner`: each row names 4 different owners; among the 32 rows of one device (aligned blocks) no owner is named more than 32 times, a bound that some block reaches.
All inputs are finite; a program needn't handle non-finite values.
Results may differ from a plain program's by a relative error of at most 0.0003.
Values sent between devices are 32-bit elements; how exact they have to be, the bound alone decides.
A program may use at most 64 MiB of HBM per device.

v0:
```python
import jax
import jax.numpy as jnp
from jax import lax
from jax.sharding import PartitionSpec as P

highest = lax.Precision.HIGHEST


def atom_weights(atom_type, channel, charge, type_table):
    type_ids = jnp.arange(type_table.shape[0], dtype=jnp.int32)
    onehot = (atom_type[:, None, :] == type_ids[None, :, None]).astype(jnp.float32)
    steric = jnp.sum(onehot * type_table[None, :, 0:1], axis=1)
    strength = jnp.sum(onehot * type_table[None, :, 1:2], axis=1)
    channels = jnp.arange(3, dtype=jnp.int32)
    pharm_part = (channel[:, None, :] == channels[None, :, None]).astype(jnp.float32) * strength[
        :, None, :
    ]
    return jnp.concatenate([steric[:, None, :], charge[:, None, :], pharm_part], axis=1)


def pair_terms(posed_xyz, atom_w, points, values, widths):
    offsets = posed_xyz[:, None, :] - points[:, :, None]
    sq_dist = jnp.sum(offsets * offsets, axis=0)
    kernel = jnp.exp(-widths[:, None, None] * sq_dist[None, :, :])
    crossed = kernel * atom_w[:, None, :]
    fields = crossed * values[:, :, None]
    intersection = jnp.sum(fields)
    scaled = jnp.sum(fields * (-2.0 * widths)[:, None, None], axis=0)
    forces = jnp.sum(scaled[None, :, :] * offsets, axis=1)
    shift_grad = jnp.sum(forces, axis=1)
    linear = jnp.sum(forces[:, None, :] * posed_xyz[None, :, :], axis=2).reshape(9)
    weight_part = jnp.sum(crossed, axis=2)
    return (jnp.concatenate([intersection[None], shift_grad, linear]), weight_part)


def local(
    coords,
    atom_type,
    channel,
    charge,
    pair_owner,
    pair_slot,
    type_table,
    widths,
    tmpl_points,
    tmpl_weights,
):
    block_count, per_block = pair_owner.shape
    atom_count = coords.shape[2]
    owners = lax.axis_size(("lib", "tmpl"))
    pair_count = block_count * per_block
    capacity = max(2, 2 * pair_count // owners)
    atom_w = atom_weights(atom_type, channel, charge, type_table)
    payload = jnp.concatenate([coords, atom_w], axis=1)
    row_count = payload.shape[1]
    payload = payload.reshape(block_count, row_count * atom_count)
    owner_ids = pair_owner.reshape(pair_count)
    slot_ids = pair_slot.reshape(pair_count)
    order_ids = jnp.arange(pair_count, dtype=jnp.int32)
    earlier = (owner_ids[None, :] == owner_ids[:, None]) & (order_ids[None, :] < order_ids[:, None])
    slot_rank = jnp.sum(earlier.astype(jnp.int32), axis=1)
    selected = (owner_ids[None, None, :] == jnp.arange(owners, dtype=jnp.int32)[:, None, None]) & (
        slot_rank[None, None, :] == jnp.arange(capacity, dtype=jnp.int32)[None, :, None]
    )
    selector = selected.astype(jnp.float32)
    by_block = jnp.sum(selector.reshape(owners, capacity, block_count, per_block), axis=3)
    outgoing = jnp.einsum("ocb,bx->ocx", by_block, payload, precision=highest).reshape(
        owners, capacity, row_count, atom_count
    )
    labels = jnp.sum(jnp.where(selected, slot_ids[None, None, :] + 1, 0), axis=2) - 1
    arrived, arrived_ids = (
        lax.all_to_all(outgoing, ("lib", "tmpl"), split_axis=0, concat_axis=0, tiled=True),
        lax.all_to_all(labels, ("lib", "tmpl"), split_axis=0, concat_axis=0, tiled=True),
    )
    received = owners * capacity
    arrived = arrived.reshape(received, row_count, atom_count)
    arrived = arrived.reshape(received // 16, 16, 8, atom_count)
    arrived_ids = arrived_ids.reshape(received // 16, 16)
    tmpl_count = tmpl_points.shape[0]
    tmpl_w = tmpl_weights.astype(jnp.float32)
    tmpl_index = jnp.arange(tmpl_count, dtype=jnp.int32)

    def process(running, element):
        batch_slots, batch_ids = element
        picker = (batch_ids[:, None] == tmpl_index[None, :]).astype(jnp.float32)
        points = jnp.einsum("gt,tcj->gcj", picker, tmpl_points, precision=highest)
        values = jnp.einsum("gt,tfj->gfj", picker, tmpl_w, precision=highest)
        results, weight_part = jax.vmap(pair_terms, in_axes=(0, 0, 0, 0, None))(
            batch_slots[:, :3], batch_slots[:, 3:], points, values, widths
        )
        running = running + jnp.einsum("gt,gfj->tfj", picker, weight_part, precision=highest)
        return (running, results)

    initial = jnp.zeros((tmpl_count, tmpl_w.shape[1], tmpl_points.shape[2]), jnp.float32)
    weight_grad, results = lax.scan(process, initial, (arrived, arrived_ids))
    results = results.reshape(owners, capacity, 13)
    results = lax.psum(results, "sub")
    returned = lax.all_to_all(results, ("lib", "tmpl"), split_axis=0, concat_axis=0, tiled=True)
    per_pair = jnp.einsum("ocp,ocx->px", selector, returned, precision=highest)
    scores = per_pair[:, 0].reshape(block_count, per_block)
    pose_grad = jnp.sum(per_pair[:, 1:].reshape(block_count, per_block, 12), axis=1)
    return (scores, pose_grad, weight_grad)


def solution(mesh):
    in_specs = (
        P(("groups", "lib", "tmpl"), None, None),
        P(("groups", "lib", "tmpl"), None),
        P(("groups", "lib", "tmpl"), None),
        P(("groups", "lib", "tmpl"), None),
        P(("groups", "lib", "tmpl"), None),
        P(("groups", "lib", "tmpl"), None),
        P(),
        P(),
        P(("lib", "tmpl"), None, "sub"),
        P(("lib", "tmpl"), None, "sub"),
    )
    out_specs = (
        P(("groups", "lib", "tmpl"), None),
        P(("groups", "lib", "tmpl"), None),
        P(("groups", "lib", "tmpl"), None, "sub"),
    )
    return jax.shard_map(local, mesh=mesh, in_specs=in_specs, out_specs=out_specs, check_vma=False)
```

profile of v0, /device:TPU:0, one launch (start us, length us, event | category | flops | bytes accessed | tf_op | source)
XLA Modules:
  0.0 232.1 jit_solution(10868090505965773083)
XLA Ops:
  3.4 7.3 %all-to-all-start = ((s32[8,1,32]{2,1,0:T(1,128)}), s32[8,1,32]{2,1,0:T(1,128)S(1)}, u32[]{:S(2)}, u32[]{:S(2)}) async-start(s32[8,1,32]{2,1,0:T(1,128)} %bitcast), calls=%async_computation | async-start | bytes 8192 | tf_op jit(solution)/shard_map/all_to_all | solution.py:73
  14.1 2.8 %fusion.21 = f32[8,32,8,128]{3,1,2,0:T(8,128)} fusion(f32[8,32,32]{2,1,0:T(8,128)S(1)} %convert_reduce_fusion, f32[32,3,128]{2,0,1:T(8,128)S(1)} %fusion.27, f32[32,1,128]{2,0,1:T(8,128)} %bitcast.85, f32[32,1,128]{2,0,1:T(8,128)S(1)} %bitcast.84, f32[32,3,128]{2,0,1:T(8,128)} %param.12), kind=kOutput, calls=%fused_computation.37 | convolution fusion | flops 100761600 | bytes 1212416 | tf_op jit(solution)/shard_map/ocb,bx->ocx/dot_general | solution.py:67
  17.1 5.8 %all-to-all-start.1 = ((f32[8,32,8,128]{3,1,2,0:T(8,128)}), f32[8,32,8,128]{3,1,2,0:T(8,128)}, u32[]{:S(2)}, u32[]{:S(2)}) async-start(f32[8,32,8,128]{3,1,2,0:T(8,128)} %fusion.21), calls=%async_computation.1 | async-start | bytes 2097152 | tf_op jit(solution)/shard_map/all_to_all | solution.py:72
  24.9 23.6 %all-to-all-done.1 = f32[8,32,8,128]{3,1,2,0:T(8,128)} async-done(((f32[8,32,8,128]{3,1,2,0:T(8,128)}), f32[8,32,8,128]{3,1,2,0:T(8,128)}, u32[]{:S(2)}, u32[]{:S(2)}) %all-to-all-start.1) | async-done | bytes 1048608 | tf_op jit(solution)/shard_map/all_to_all | solution.py:72
  48.5 2.8 %copy.91 = f32[8,32,8,128]{3,2,1,0:T(8,128)} copy(f32[8,32,8,128]{3,1,2,0:T(8,128)} %all-to-all-done.1) | data formatting | bytes 2097152 | tf_op jit(solution)/shard_map/all_to_all | solution.py:72
  51.3 163.1 %while.14 = (s32[]{:T(128)}, f32[512,5,128]{2,0,1:T(8,128)S(1)}, f32[16,16,13]{2,1,0:T(8,128)}, s32[16,16]{1,0:T(8,128)S(1)}, f32[1,5,1,1]{1,3,2,0:T(1,128)S(1)}...) while((s32[]{:T(128)}, f32[512,5,128]{2,0,1:T(8,128)S(1)}, ...), condition=%wide.region_13.14_spmd.clone, body=%wide.region_5.13_spmd.clone.sunk | while | flops 178434272 | bytes 9821583 | solution.py:95
  54.2 3.6 %fusion.53 = (f32[16]{0:T(128)S(1)}, f32[16,128,128]{2,1,0:T(8,128)S(1)}, f32[16,5,128]{2,1,0:T(8,128)S(1)}) fusion(f32[16,5,128]{2,1,0:T(8,128)S(1)} %copy.119, f32[16,5,128]{2,1,0:T(8,128)S(1)} %slice.35, f32[16,128,128]{2,1,0:T(8,128)S(1)} %fusion.52, f32[5]{0:T(128)S(1)} %bitcast.87, f32[5]{0:T(128)S(1)} %broadcast_multiply_fusion.2), kind=kLoop, calls=%fused_computation.5.clone.1 | loop fusion | flops 8902640 | bytes 2220136 | tf_op jit(solution)/shard_map/while/body/eval_jaxpr/vmap()/reduce_sum | solution.py:27
  57.8 1.6 fusion.54
  64.4 3.6 %fusion.53 = (f32[16]{0:T(128)S(1)}, f32[16,128,128]{2,1,0:T(8,128)S(1)}, f32[16,5,128]{2,1,0:T(8,128)S(1)}) fusion(f32[16,5,128]{2,1,0:T(8,128)S(1)} %copy.119, f32[16,5,128]{2,1,0:T(8,128)S(1)} %slice.35, f32[16,128,128]{2,1,0:T(8,128)S(1)} %fusion.52, f32[5]{0:T(128)S(1)} %bitcast.87, f32[5]{0:T(128)S(1)} %broadcast_multiply_fusion.2), kind=kLoop, calls=%fused_computation.5.clone.1 | loop fusion | flops 8902640 | bytes 2220136 | tf_op jit(solution)/shard_map/while/body/eval_jaxpr/vmap()/reduce_sum | solution.py:27
  68.0 1.6 fusion.54
  70.5 1.1 convolution_add_fusion.2
  74.6 3.6 %fusion.53 = (f32[16]{0:T(128)S(1)}, f32[16,128,128]{2,1,0:T(8,128)S(1)}, f32[16,5,128]{2,1,0:T(8,128)S(1)}) fusion(f32[16,5,128]{2,1,0:T(8,128)S(1)} %copy.119, f32[16,5,128]{2,1,0:T(8,128)S(1)} %slice.35, f32[16,128,128]{2,1,0:T(8,128)S(1)} %fusion.52, f32[5]{0:T(128)S(1)} %bitcast.87, f32[5]{0:T(128)S(1)} %broadcast_multiply_fusion.2), kind=kLoop, calls=%fused_computation.5.clone.1 | loop fusion | flops 8902640 | bytes 2220136 | tf_op jit(solution)/shard_map/while/body/eval_jaxpr/vmap()/reduce_sum | solution.py:27
  78.2 1.6 fusion.54
  84.8 3.6 %fusion.53 = (f32[16]{0:T(128)S(1)}, f32[16,128,128]{2,1,0:T(8,128)S(1)}, f32[16,5,128]{2,1,0:T(8,128)S(1)}) fusion(f32[16,5,128]{2,1,0:T(8,128)S(1)} %copy.119, f32[16,5,128]{2,1,0:T(8,128)S(1)} %slice.35, f32[16,128,128]{2,1,0:T(8,128)S(1)} %fusion.52, f32[5]{0:T(128)S(1)} %bitcast.87, f32[5]{0:T(128)S(1)} %broadcast_multiply_fusion.2), kind=kLoop, calls=%fused_computation.5.clone.1 | loop fusion | flops 8902640 | bytes 2220136 | tf_op jit(solution)/shard_map/while/body/eval_jaxpr/vmap()/reduce_sum | solution.py:27
  88.4 1.6 fusion.54
  90.9 1.1 convolution_add_fusion.2
  95.0 3.6 %fusion.53 = (f32[16]{0:T(128)S(1)}, f32[16,128,128]{2,1,0:T(8,128)S(1)}, f32[16,5,128]{2,1,0:T(8,128)S(1)}) fusion(f32[16,5,128]{2,1,0:T(8,128)S(1)} %copy.119, f32[16,5,128]{2,1,0:T(8,128)S(1)} %slice.35, f32[16,128,128]{2,1,0:T(8,128)S(1)} %fusion.52, f32[5]{0:T(128)S(1)} %bitcast.87, f32[5]{0:T(128)S(1)} %broadcast_multiply_fusion.2), kind=kLoop, calls=%fused_computation.5.clone.1 | loop fusion | flops 8902640 | bytes 2220136 | tf_op jit(solution)/shard_map/while/body/eval_jaxpr/vmap()/reduce_sum | solution.py:27
  98.6 1.6 fusion.54
  101.1 1.1 convolution_add_fusion.2
  105.2 3.6 %fusion.53 = (f32[16]{0:T(128)S(1)}, f32[16,128,128]{2,1,0:T(8,128)S(1)}, f32[16,5,128]{2,1,0:T(8,128)S(1)}) fusion(f32[16,5,128]{2,1,0:T(8,128)S(1)} %copy.119, f32[16,5,128]{2,1,0:T(8,128)S(1)} %slice.35, f32[16,128,128]{2,1,0:T(8,128)S(1)} %fusion.52, f32[5]{0:T(128)S(1)} %bitcast.87, f32[5]{0:T(128)S(1)} %broadcast_multiply_fusion.2), kind=kLoop, calls=%fused_computation.5.clone.1 | loop fusion | flops 8902640 | bytes 2220136 | tf_op jit(solution)/shard_map/while/body/eval_jaxpr/vmap()/reduce_sum | solution.py:27
  108.8 1.6 fusion.54
  115.4 3.6 %fusion.53 = (f32[16]{0:T(128)S(1)}, f32[16,128,128]{2,1,0:T(8,128)S(1)}, f32[16,5,128]{2,1,0:T(8,128)S(1)}) fusion(f32[16,5,128]{2,1,0:T(8,128)S(1)} %copy.119, f32[16,5,128]{2,1,0:T(8,128)S(1)} %slice.35, f32[16,128,128]{2,1,0:T(8,128)S(1)} %fusion.52, f32[5]{0:T(128)S(1)} %bitcast.87, f32[5]{0:T(128)S(1)} %broadcast_multiply_fusion.2), kind=kLoop, calls=%fused_computation.5.clone.1 | loop fusion | flops 8902640 | bytes 2220136 | tf_op jit(solution)/shard_map/while/body/eval_jaxpr/vmap()/reduce_sum | solution.py:27
  118.9 1.6 fusion.54
  121.5 1.1 convolution_add_fusion.2
  125.6 3.6 %fusion.53 = (f32[16]{0:T(128)S(1)}, f32[16,128,128]{2,1,0:T(8,128)S(1)}, f32[16,5,128]{2,1,0:T(8,128)S(1)}) fusion(f32[16,5,128]{2,1,0:T(8,128)S(1)} %copy.119, f32[16,5,128]{2,1,0:T(8,128)S(1)} %slice.35, f32[16,128,128]{2,1,0:T(8,128)S(1)} %fusion.52, f32[5]{0:T(128)S(1)} %bitcast.87, f32[5]{0:T(128)S(1)} %broadcast_multiply_fusion.2), kind=kLoop, calls=%fused_computation.5.clone.1 | loop fusion | flops 8902640 | bytes 2220136 | tf_op jit(solution)/shard_map/while/body/eval_jaxpr/vmap()/reduce_sum | solution.py:27
  129.1 1.6 fusion.54
  135.7 3.6 %fusion.53 = (f32[16]{0:T(128)S(1)}, f32[16,128,128]{2,1,0:T(8,128)S(1)}, f32[16,5,128]{2,1,0:T(8,128)S(1)}) fusion(f32[16,5,128]{2,1,0:T(8,128)S(1)} %copy.119, f32[16,5,128]{2,1,0:T(8,128)S(1)} %slice.35, f32[16,128,128]{2,1,0:T(8,128)S(1)} %fusion.52, f32[5]{0:T(128)S(1)} %bitcast.87, f32[5]{0:T(128)S(1)} %broadcast_multiply_fusion.2), kind=kLoop, calls=%fused_computation.5.clone.1 | loop fusion | flops 8902640 | bytes 2220136 | tf_op jit(solution)/shard_map/while/body/eval_jaxpr/vmap()/reduce_sum | solution.py:27
  139.3 1.6 fusion.54
  145.9 3.6 %fusion.53 = (f32[16]{0:T(128)S(1)}, f32[16,128,128]{2,1,0:T(8,128)S(1)}, f32[16,5,128]{2,1,0:T(8,128)S(1)}) fusion(f32[16,5,128]{2,1,0:T(8,128)S(1)} %copy.119, f32[16,5,128]{2,1,0:T(8,128)S(1)} %slice.35, f32[16,128,128]{2,1,0:T(8,128)S(1)} %fusion.52, f32[5]{0:T(128)S(1)} %bitcast.87, f32[5]{0:T(128)S(1)} %broadcast_multiply_fusion.2), kind=kLoop, calls=%fused_computation.5.clone.1 | loop fusion | flops 8902640 | bytes 2220136 | tf_op jit(solution)/shard_map/while/body/eval_jaxpr/vmap()/reduce_sum | solution.py:27
  149.5 1.6 fusion.54
  156.1 3.6 %fusion.53 = (f32[16]{0:T(128)S(1)}, f32[16,128,128]{2,1,0:T(8,128)S(1)}, f32[16,5,128]{2,1,0:T(8,128)S(1)}) fusion(f32[16,5,128]{2,1,0:T(8,128)S(1)} %copy.119, f32[16,5,128]{2,1,0:T(8,128)S(1)} %slice.35, f32[16,128,128]{2,1,0:T(8,128)S(1)} %fusion.52, f32[5]{0:T(128)S(1)} %bitcast.87, f32[5]{0:T(128)S(1)} %broadcast_multiply_fusion.2), kind=kLoop, calls=%fused_computation.5.clone.1 | loop fusion | flops 8902640 | bytes 2220136 | tf_op jit(solution)/shard_map/while/body/eval_jaxpr/vmap()/reduce_sum | solution.py:27
  159.7 1.6 fusion.54
  162.2 1.1 convolution_add_fusion.2
  166.3 3.6 %fusion.53 = (f32[16]{0:T(128)S(1)}, f32[16,128,128]{2,1,0:T(8,128)S(1)}, f32[16,5,128]{2,1,0:T(8,128)S(1)}) fusion(f32[16,5,128]{2,1,0:T(8,128)S(1)} %copy.119, f32[16,5,128]{2,1,0:T(8,128)S(1)} %slice.35, f32[16,128,128]{2,1,0:T(8,128)S(1)} %fusion.52, f32[5]{0:T(128)S(1)} %bitcast.87, f32[5]{0:T(128)S(1)} %broadcast_multiply_fusion.2), kind=kLoop, calls=%fused_computation.5.clone.1 | loop fusion | flops 8902640 | bytes 2220136 | tf_op jit(solution)/shard_map/while/body/eval_jaxpr/vmap()/reduce_sum | solution.py:27
  169.9 1.6 fusion.54
  172.4 1.1 convolution_add_fusion.2
  176.5 3.6 %fusion.53 = (f32[16]{0:T(128)S(1)}, f32[16,128,128]{2,1,0:T(8,128)S(1)}, f32[16,5,128]{2,1,0:T(8,128)S(1)}) fusion(f32[16,5,128]{2,1,0:T(8,128)S(1)} %copy.119, f32[16,5,128]{2,1,0:T(8,128)S(1)} %slice.35, f32[16,128,128]{2,1,0:T(8,128)S(1)} %fusion.52, f32[5]{0:T(128)S(1)} %bitcast.87, f32[5]{0:T(128)S(1)} %broadcast_multiply_fusion.2), kind=kLoop, calls=%fused_computation.5.clone.1 | loop fusion | flops 8902640 | bytes 2220136 | tf_op jit(solution)/shard_map/while/body/eval_jaxpr/vmap()/reduce_sum | solution.py:27
  180.1 1.6 fusion.54
  182.6 1.1 convolution_add_fusion.2
  186.7 3.6 %fusion.53 = (f32[16]{0:T(128)S(1)}, f32[16,128,128]{2,1,0:T(8,128)S(1)}, f32[16,5,128]{2,1,0:T(8,128)S(1)}) fusion(f32[16,5,128]{2,1,0:T(8,128)S(1)} %copy.119, f32[16,5,128]{2,1,0:T(8,128)S(1)} %slice.35, f32[16,128,128]{2,1,0:T(8,128)S(1)} %fusion.52, f32[5]{0:T(128)S(1)} %bitcast.87, f32[5]{0:T(128)S(1)} %broadcast_multiply_fusion.2), kind=kLoop, calls=%fused_computation.5.clone.1 | loop fusion | flops 8902640 | bytes 2220136 | tf_op jit(solution)/shard_map/while/body/eval_jaxpr/vmap()/reduce_sum | solution.py:27
  190.3 1.6 fusion.54
  196.9 3.6 %fusion.53 = (f32[16]{0:T(128)S(1)}, f32[16,128,128]{2,1,0:T(8,128)S(1)}, f32[16,5,128]{2,1,0:T(8,128)S(1)}) fusion(f32[16,5,128]{2,1,0:T(8,128)S(1)} %copy.119, f32[16,5,128]{2,1,0:T(8,128)S(1)} %slice.35, f32[16,128,128]{2,1,0:T(8,128)S(1)} %fusion.52, f32[5]{0:T(128)S(1)} %bitcast.87, f32[5]{0:T(128)S(1)} %broadcast_multiply_fusion.2), kind=kLoop, calls=%fused_computation.5.clone.1 | loop fusion | flops 8902640 | bytes 2220136 | tf_op jit(solution)/shard_map/while/body/eval_jaxpr/vmap()/reduce_sum | solution.py:27
  200.5 1.6 fusion.54
  207.1 3.6 %fusion.53 = (f32[16]{0:T(128)S(1)}, f32[16,128,128]{2,1,0:T(8,128)S(1)}, f32[16,5,128]{2,1,0:T(8,128)S(1)}) fusion(f32[16,5,128]{2,1,0:T(8,128)S(1)} %copy.119, f32[16,5,128]{2,1,0:T(8,128)S(1)} %slice.35, f32[16,128,128]{2,1,0:T(8,128)S(1)} %fusion.52, f32[5]{0:T(128)S(1)} %bitcast.87, f32[5]{0:T(128)S(1)} %broadcast_multiply_fusion.2), kind=kLoop, calls=%fused_computation.5.clone.1 | loop fusion | flops 8902640 | bytes 2220136 | tf_op jit(solution)/shard_map/while/body/eval_jaxpr/vmap()/reduce_sum | solution.py:27
  210.7 1.6 fusion.54
  214.4 1.2 copy.93
  215.5 3.6 %psum.7 = f32[8,32,13]{1,2,0:T(8,128)S(1)} all-reduce(f32[8,32,13]{1,2,0:T(8,128)S(1)} %copy.93), channel_id=1, replica_groups=mesh['groups'=2,'lib'=4,'tmpl'=2,'sub'=2] {'sub'}, use_global_device_ids=true, to_apply=%region_14.15 | all-reduce | flops 3328 | bytes 26624 | tf_op jit(solution)/shard_map/psum | solution.py:97
  219.2 9.7 %all_to_all.16 = f32[8,1,416]{2,1,0:T(1,128)S(1)} all-to-all(f32[8,1,416]{2,1,0:T(1,128)S(1)} %reshape.162), channel_id=1, replica_groups=mesh['groups'=2,'lib'=4,'tmpl'=2,'sub'=2] {'lib','tmpl'}, dimensions={0} | all-to-all | bytes 26624 | tf_op jit(solution)/shard_map/all_to_all | solution.py:98
  (343 shorter events, 82.2 us)
Async XLA Ops:
  3.4 13.7 %all-to-all-start = ((s32[8,1,32]{2,1,0:T(1,128)}), s32[8,1,32]{2,1,0:T(1,128)S(1)}, u32[]{:S(2)}, u32[]{:S(2)}) async-start(s32[8,1,32]{2,1,0:T(1,128)} %bitcast), calls=%async_computation | async-start | bytes 8192 | tf_op jit(solution)/shard_map/all_to_all | solution.py:73
  16.8 6.2 %copy-start.2 = (bf16[512,5,128]{2,0,1:T(8,128)(2,1)S(1)}, bf16[512,5,128]{2,0,1:T(8,128)(2,1)}, u32[]{:S(2)}) copy-start(bf16[512,5,128]{2,0,1:T(8,128)(2,1)} %param.21) | copy-start | bytes 1966084
  17.1 31.4 %all-to-all-start.1 = ((f32[8,32,8,128]{3,1,2,0:T(8,128)}), f32[8,32,8,128]{3,1,2,0:T(8,128)}, u32[]{:S(2)}, u32[]{:S(2)}) async-start(f32[8,32,8,128]{3,1,2,0:T(8,128)} %fusion.21), calls=%async_computation.1 | async-start | bytes 2097152 | tf_op jit(solution)/shard_map/all_to_all | solution.py:72
  22.9 0.7 copy-start.3
  23.1 28.2 %copy-start.1 = (f32[512,3,128]{2,0,1:T(8,128)S(1)}, f32[512,3,128]{2,0,1:T(8,128)}, u32[]{:S(2)}) copy-start(f32[512,3,128]{2,0,1:T(8,128)} %param.20) | copy-start | bytes 2359300
  214.3 17.7 %copy-start = (f32[512,5,128]{2,0,1:T(8,128)}, f32[512,5,128]{2,0,1:T(8,128)S(1)}, u32[]{:S(2)}) copy-start(f32[512,5,128]{2,0,1:T(8,128)S(1)} %get-tuple-element.152) | copy-start | bytes 3932164
where the time goes:
time: 233 us; the launch traced here: 232 us
  other arithmetic  107 us (46%)
  local copies, waits for them, and re-layouts  36.5 us (16%)
  matrix products  36.1 us (15%)
  waiting for transfers between devices  23.9 us (10%)
  blocking collectives  13.3 us (6%)
  starting transfers between devices  13.1 us (6%)
    reduce_sum x16, other arithmetic, pair_terms(): intersection = jnp.sum(fields)  57.4 us
    reduce_sum x16, other arithmetic, pair_terms(): shift_grad = jnp.sum(forces, axis=1)  25.2 us
    all_to_all x1, waiting for transfers between devices, local(): lax.all_to_all(outgoing, ('lib', 'tmpl'), split_axis=0, concat_axis=0, ti...  23.6 us
    dot_general x16, matrix products, process(): jnp.einsum('gt,gfj->tfj', picker, weight_part, precision=highest)  18.2 us
    reduce_sum x16, other arithmetic, pair_terms(): sq_dist = jnp.sum(offsets * offsets, axis=0)  16.6 us
    squeeze x16, local copies, waits for them, and re-layouts, local(): weight_grad, results = lax.scan(process, initial, (arrived, arrived_ids))  13.6 us
    all_to_all x1, blocking collectives, local(): lax.all_to_all(results, ('lib', 'tmpl'), split_axis=0, concat_axis=0, til...  9.74 us
    dynamic_update_slice x16, local copies, waits for them, and re-layouts, local(): weight_grad, results = lax.scan(process, initial, (arrived, arrived_ids))  9.65 us
  transfers between devices with their start and end apart: 2, of which 2 were waited for; matrix products, arithmetic and copies ran while one was open for 3% of the time, Pallas kernels for 0%

commit v1 on v0

v1 whole, which is shorter than its diff:
```python
import functools
import math

import jax
import jax.numpy as jnp
from jax import lax
from jax.experimental import pallas as pl
from jax.experimental.pallas import tpu as pltpu
from jax.sharding import PartitionSpec as P

MESH = pl.DeviceIdType.MESH
F32 = jnp.float32
BF16 = jnp.bfloat16
GROUP = 4
VALUES = 16


def gather_kernel(libs, tmpls, own_ref, all_ref, local_sem, z_send, z_recv, x_send, x_recv, s_send, s_recv):
    l = lax.axis_index("lib")
    t = lax.axis_index("tmpl")
    s = lax.axis_index("sub")
    half = own_ref.shape[0] // 2
    barrier = pltpu.get_barrier_semaphore()

    @pl.loop(1, libs)
    def _(k):
        pl.semaphore_signal(barrier, inc=1, device_id={"lib": lax.rem(l + k, libs)}, device_id_type=MESH)

    @pl.loop(1, tmpls)
    def _(k):
        pl.semaphore_signal(barrier, inc=1, device_id={"tmpl": lax.rem(t + k, tmpls)}, device_id_type=MESH)

    pl.semaphore_signal(barrier, inc=1, device_id={"sub": 1 - s}, device_id_type=MESH)
    mine = own_ref.at[pl.ds(s * half, half)]
    local = pltpu.make_async_copy(own_ref, all_ref.at[l, t], local_sem)
    pl.semaphore_wait(barrier, libs + tmpls - 1)
    local.start()

    def z_copy(k):
        return pltpu.make_async_remote_copy(
            src_ref=mine, dst_ref=all_ref.at[l, t, pl.ds(s * half, half)], send_sem=z_send.at[k], recv_sem=z_recv.at[k],
            device_id={"lib": lax.rem(l + k, libs)}, device_id_type=MESH)

    def x_copy(k, m, src):
        return pltpu.make_async_remote_copy(
            src_ref=src, dst_ref=all_ref.at[lax.rem(l - k + libs, libs), t, pl.ds(s * half, half)],
            send_sem=x_send.at[k, m], recv_sem=x_recv.at[k, m],
            device_id={"tmpl": lax.rem(t + m, tmpls)}, device_id_type=MESH)

    def s_copy(k, m):
        spot = all_ref.at[lax.rem(l - k + libs, libs), lax.rem(t - m + tmpls, tmpls), pl.ds(s * half, half)]
        return pltpu.make_async_remote_copy(
            src_ref=spot, dst_ref=spot, send_sem=s_send.at[k, m], recv_sem=s_recv.at[k, m],
            device_id={"sub": 1 - s}, device_id_type=MESH)

    @pl.loop(1, tmpls)
    def _(m):
        x_copy(0, m, mine).start()

    @pl.loop(1, libs)
    def _(k):
        z_copy(k).start()

    @pl.loop(1, libs)
    def _(k):
        z_copy(k).wait_recv()
        spot = all_ref.at[lax.rem(l - k + libs, libs), t, pl.ds(s * half, half)]

        @pl.loop(1, tmpls)
        def _(m):
            x_copy(k, m, spot).start()

        s_copy(k, 0).start()

    @pl.loop(1, tmpls)
    def _(m):
        @pl.loop(0, libs)
        def _(k):
            x_copy(k, m, mine).wait_recv()
            s_copy(k, m).start()

    local.wait()

    @pl.loop(1, libs)
    def _(k):
        z_copy(k).wait_send()
        s_copy(k, 0).wait()

    @pl.loop(1, tmpls)
    def _(m):
        @pl.loop(0, libs)
        def _(k):
            x_copy(k, m, mine).wait_send()
            s_copy(k, m).wait()


def gather_blocks(payload, libs, tmpls):
    dma = pltpu.SemaphoreType.DMA
    return pl.pallas_call(
        functools.partial(gather_kernel, libs, tmpls),
        out_shape=jax.ShapeDtypeStruct((libs, tmpls) + payload.shape, F32),
        in_specs=[pl.BlockSpec(memory_space=pltpu.VMEM)],
        out_specs=pl.BlockSpec(memory_space=pltpu.VMEM),
        scratch_shapes=[dma, dma((libs,)), dma((libs,)), dma((libs, tmpls)), dma((libs, tmpls)),
                        dma((libs, tmpls)), dma((libs, tmpls))],
        compiler_params=pltpu.CompilerParams(collective_id=0, has_side_effects=True, vmem_limit_bytes=60 << 20),
    )(payload)


def split3(a):
    h = a.astype(BF16).astype(F32)
    r = a - h
    m = r.astype(BF16).astype(F32)
    return h, m, r - m


def split2(a):
    h = a.astype(BF16)
    return h, (a - h.astype(F32)).astype(BF16)


def pair_kernel(per_dev, slot_ref, widths_ref, blocks_ref, points_ref, weights_ref, wg_ref, out_ref, res_ref):
    devices = blocks_ref.shape[0]
    wg_ref[...] = jnp.zeros_like(wg_ref)
    res_ref[...] = jnp.zeros_like(res_ref)
    row = lax.broadcasted_iota(jnp.int32, (8, 128), 0)
    row16 = lax.broadcasted_iota(jnp.int32, (VALUES, 128), 0)
    lane16 = lax.broadcasted_iota(jnp.int32, (VALUES, 128), 1)
    low = row < 4
    log2e = math.log2(math.e)
    wide = [widths_ref[f] for f in range(5)]
    scale = [-log2e * w for w in wide]

    def one(dev, b, slot):
        valid = jnp.where(slot >= 0, F32(1), F32(0))
        slot = jnp.maximum(slot, 0)
        x = [jnp.broadcast_to(blocks_ref[dev, b, pl.ds(c, 1), :], (8, 128)) for c in range(3)]
        y = [jnp.broadcast_to(points_ref[slot, pl.ds(c, 1), :], (8, 128)) for c in range(3)]

        def rows(first, norm_row, one_row, p):
            norm = p[0] * p[0] + p[1] * p[1] + p[2] * p[2]
            v = jnp.where(row == 0, p[0] * first, jnp.where(row == 1, p[1] * first, p[2] * first))
            return jnp.where(row < 3, v, jnp.where(row == norm_row, norm, jnp.where(row == one_row, 1.0, 0.0)))

        xh, xm, xl = split3(rows(1.0, 3, 4, x))
        yh, ym, yl = split3(rows(-2.0, 4, 3, y))
        xs = jnp.concatenate([xh, xh, xh, xm, xm, xl], axis=0).astype(BF16)
        ys = jnp.concatenate([yh, ym, yl, yh, ym, yh], axis=0).astype(BF16)
        dist = lax.dot_general(ys, xs, (((0,), (0,)), ((), ())), preferred_element_type=F32)
        chan = blocks_ref[dev, b, pl.ds(6, 1), :]
        steric = blocks_ref[dev, b, pl.ds(3, 1), :] * valid
        charge = blocks_ref[dev, b, pl.ds(4, 1), :] * valid
        strength = blocks_ref[dev, b, pl.ds(5, 1), :] * valid
        pharm_scale = jnp.where(chan == 0.0, scale[2], jnp.where(chan == 1.0, scale[3], scale[4]))
        inner = jnp.where(row % 4 == 0, 1.0, jnp.where(row % 4 == 1, x[0], jnp.where(row % 4 == 2, x[1], x[2])))
        outer = jnp.concatenate([jnp.where(low, 1.0, x[0]), jnp.where(low, x[1], x[2])], axis=0)
        moments = outer * jnp.concatenate([inner, inner], axis=0)

        def contract(exps, coefs):
            hi, lo = split2(exps)
            rhs = jnp.concatenate([hi, lo], axis=1)
            lhs = jnp.concatenate([moments * c for c in coefs], axis=0)
            lh, ll = split2(lhs)
            lhs2 = jnp.concatenate([lh, ll], axis=0)
            lhs2 = jnp.concatenate([lhs2, lhs2], axis=1)
            got = lax.dot_general(lhs2, rhs, (((1,), (1,)), ((), ())), preferred_element_type=F32)
            n = VALUES * len(coefs)
            got = got[:n] + got[n:]
            return [got[VALUES * c:VALUES * (c + 1)] for c in range(len(coefs))]

        parts = contract(jnp.exp2(dist * scale[0]), [steric]) + contract(jnp.exp2(dist * scale[1]), [charge])
        parts += contract(jnp.exp2(dist * pharm_scale),
                          [jnp.where(chan == float(c), strength, 0.0) for c in range(3)])
        vals = weights_ref[slot].astype(F32)
        total = jnp.zeros((VALUES, 128), F32)
        score = jnp.zeros((1, 128), F32)
        for f in range(5):
            v = vals[f:f + 1]
            score = score + v * parts[f][0:1]
            total = total + (v * (-2.0 * wide[f])) * parts[f]
        base = jnp.concatenate([total[0:4]] * 4, axis=0)
        y16 = jnp.concatenate([jnp.where(low, 0.0, y[0]), jnp.where(low, y[1], y[2])], axis=0)
        final = jnp.where(row16 == 0, score, total - y16 * base)
        summed = jnp.sum(final, axis=1, keepdims=True)
        wpart = jnp.concatenate([p[0:1] for p in parts], axis=0)
        return slot, wpart, summed

    group = math.gcd(GROUP, per_dev)

    @pl.loop(0, devices)
    def _(dev):
        @pl.loop(0, per_dev // group)
        def _(g):
            slots = [slot_ref[dev * per_dev + g * group + u] for u in range(group)]
            best = slots[0]
            for v in slots[1:]:
                best = jnp.maximum(best, v)

            @pl.when(best >= 0)
            def _():
                done = [one(dev, g * group + u, slots[u]) for u in range(group)]
                for u, (slot, wpart, summed) in enumerate(done):
                    wg_ref[slot] += wpart
                acc = res_ref[dev]
                for u, (slot, wpart, summed) in enumerate(done):
                    acc = jnp.where(lane16 == g * group + u, summed, acc)
                res_ref[dev] = acc

    @pl.loop(0, devices)
    def _(dev):
        r = res_ref[dev]
        packed = r[0:4]
        for q in range(1, 4):
            packed = packed + pltpu.roll(r[4 * q:4 * q + 4], 32 * q, 1)
        out_ref[dev] = packed


def run_pairs(slots, widths, blocks, points, weights):
    tmpl_count = points.shape[0]
    devices, per_dev = blocks.shape[:2]
    vmem = pl.BlockSpec(memory_space=pltpu.VMEM)
    smem = pl.BlockSpec(memory_space=pltpu.SMEM)
    return pl.pallas_call(
        functools.partial(pair_kernel, per_dev),
        out_shape=(jax.ShapeDtypeStruct((tmpl_count, 5, 128), F32), jax.ShapeDtypeStruct((devices, 4, 128), F32)),
        in_specs=[smem, smem, vmem, vmem, vmem],
        out_specs=(vmem, vmem),
        scratch_shapes=[pltpu.VMEM((devices, VALUES, 128), F32)],
        compiler_params=pltpu.CompilerParams(vmem_limit_bytes=60 << 20),
    )(slots, widths, blocks, points, weights)


def return_kernel(libs, tmpls, res_ref, owner_ref, score_ref, pose_ref, got_ref, local_sem, send_sem, recv_sem):
    l = lax.axis_index("lib")
    t = lax.axis_index("tmpl")
    s = lax.axis_index("sub")
    owners = libs * tmpls
    count = 2 * owners
    me = (l * tmpls + t) * 2 + s
    barrier = pltpu.get_barrier_semaphore()

    def peer(k):
        other = lax.rem(me + k, count)
        return other // 2, {"lib": other // (2 * tmpls), "tmpl": lax.rem(other // 2, tmpls), "sub": lax.rem(other, 2)}

    @pl.loop(1, count)
    def _(k):
        pl.semaphore_signal(barrier, inc=1, device_id=peer(k)[1], device_id_type=MESH)

    local = pltpu.make_async_copy(res_ref.at[l * tmpls + t], got_ref.at[me], local_sem)
    local.start()
    pl.semaphore_wait(barrier, count - 1)

    def copy(k):
        block, where = peer(k)
        return pltpu.make_async_remote_copy(
            src_ref=res_ref.at[block], dst_ref=got_ref.at[me], send_sem=send_sem.at[k], recv_sem=recv_sem.at[k],
            device_id=where, device_id_type=MESH)

    @pl.loop(1, count)
    def _(k):
        copy(k).start()

    local.wait()

    @pl.loop(1, count)
    def _(k):
        copy(k).wait()

    owner = owner_ref[...]

    def add(o, carry):
        total, scores = carry
        both = got_ref[2 * o] + got_ref[2 * o + 1]
        scores = jnp.where(owner == o, jnp.broadcast_to(both[0:1], (8, 128)), scores)
        return total + both, scores

    total, scores = lax.fori_loop(0, owners, add, (jnp.zeros((4, 128), F32), jnp.zeros((8, 128), F32)))
    rows = [total] + [pltpu.roll(total, 128 - 32 * q, 1) for q in range(1, 4)]
    pose = jnp.concatenate([rows[1][0:1], rows[2][0:1], rows[3][0:1], rows[1][1:4], rows[2][1:4], rows[3][1:4],
                            jnp.zeros((4, 128), F32)], axis=0)
    blocks = score_ref.shape[0]
    score_ref[...] = scores.T[:blocks, :score_ref.shape[1]]
    pose_ref[...] = pose.T[:blocks, :12]


def send_back(res, owner_rows, blocks, per_block, libs, tmpls):
    dma = pltpu.SemaphoreType.DMA
    count = 2 * libs * tmpls
    vmem = pl.BlockSpec(memory_space=pltpu.VMEM)
    return pl.pallas_call(
        functools.partial(return_kernel, libs, tmpls),
        out_shape=(jax.ShapeDtypeStruct((blocks, per_block), F32), jax.ShapeDtypeStruct((blocks, 12), F32)),
        in_specs=[vmem, vmem],
        out_specs=(vmem, vmem),
        scratch_shapes=[pltpu.VMEM((count, 4, 128), F32), dma, dma((count,)), dma((count,))],
        compiler_params=pltpu.CompilerParams(collective_id=1, has_side_effects=True),
    )(res, owner_rows)


def local(libs, tmpls, coords, atom_type, channel, charge, pair_owner, pair_slot, type_table, widths, tmpl_points,
          tmpl_weights):
    blocks, per_block = pair_owner.shape
    tmpl_count = tmpl_points.shape[0]
    types = jnp.arange(type_table.shape[0], dtype=jnp.int32)
    hot = atom_type[:, None, :] == types[None, :, None]
    steric = jnp.sum(jnp.where(hot, type_table[None, :, 0:1], 0.0), axis=1)
    strength = jnp.sum(jnp.where(hot, type_table[None, :, 1:2], 0.0), axis=1)
    names = jnp.pad((pair_owner * tmpl_count + pair_slot).astype(F32), ((0, 0), (0, 128 - per_block)))
    payload = jnp.stack([coords[:, 0], coords[:, 1], coords[:, 2], steric, charge, strength, channel.astype(F32), names],
                        axis=1)
    gathered = gather_blocks(payload, libs, tmpls).reshape(libs * tmpls, blocks, 8, 128)
    me = lax.axis_index("lib") * tmpls + lax.axis_index("tmpl")
    ids = gathered[:, :, 7, :per_block].astype(jnp.int32) - me * tmpl_count
    slots = jnp.max(jnp.where((ids >= 0) & (ids < tmpl_count), ids, -1), axis=2).reshape(-1)
    weight_grad, res = run_pairs(slots, widths, gathered, tmpl_points, tmpl_weights)
    owner_rows = jnp.pad(pair_owner.T, ((0, 8 - per_block), (0, 128 - blocks)), constant_values=-1)
    scores, pose = send_back(res, owner_rows, blocks, per_block, libs, tmpls)
    return scores, pose, weight_grad


def solution(mesh):
    every = ("groups", "lib", "tmpl")
    in_specs = (P(every, None, None), P(every, None), P(every, None), P(every, None), P(every, None), P(every, None),
                P(), P(), P(("lib", "tmpl"), None, "sub"), P(("lib", "tmpl"), None, "sub"))
    out_specs = (P(every, None), P(every, None), P(every, None, "sub"))
    body = functools.partial(local, mesh.shape["lib"], mesh.shape["tmpl"])
    return jax.shard_map(body, mesh=mesh, in_specs=in_specs, out_specs=out_specs, check_vma=False)
```

time: 233 us -> 115 us (0.49)
  other arithmetic: 107 us -> 3.93 us
  Pallas kernels: 0 us -> 97 us
  matrix products: 36.1 us -> 0 us
  waiting for transfers between devices: 23.9 us -> 0 us
  local copies, waits for them, and re-layouts: 36.5 us -> 13.1 us
  blocking collectives: 13.3 us -> 0 us
  starting transfers between devices: 13.1 us -> 0 us
    reduce_sum x69 -> x1, other arithmetic: 102 us -> 0.89 us  [local(): strength = jnp.sum(jnp.where(hot, type_table[None, :, 1:2], 0.0), axis=1)]
    pallas_call x0 -> x3, Pallas kernels: none -> 97 us  [the longest x1 70.4 us: run_pairs(): pl.pallas_call(functools.partial(pair_kernel, per_dev), out_shape=(jax.Sh...]
    dot_general x50 -> x0, matrix products: 36.1 us -> none  [the longest x16 18.2 us: process(): jnp.einsum('gt,gfj->tfj', picker, weight_part, precision=highest)]
    all_to_all x2 -> x0, waiting for transfers between devices: 23.9 us -> none  [the longest x1 23.6 us: local(): lax.all_to_all(outgoing, ('lib', 'tmpl'), split_axis=0, concat_axis=0, ti...]
    squeeze x16 -> x0, local copies, waits for them, and re-layouts: 13.6 us -> none  [local(): weight_grad, results = lax.scan(process, initial, (arrived, arrived_ids))]
    all_to_all x2 -> x0, starting transfers between devices: 13.1 us -> none  [the longest x1 7.28 us: local(): lax.all_to_all(labels, ('lib', 'tmpl'), split_axis=0, concat_axis=0, tile...]
    all_to_all x1 -> x0, blocking collectives: 9.74 us -> none  [local(): lax.all_to_all(results, ('lib', 'tmpl'), split_axis=0, concat_axis=0, til...]
    dynamic_update_slice x16 -> x0, local copies, waits for them, and re-layouts: 9.65 us -> none  [local(): weight_grad, results = lax.scan(process, initial, (arrived, arrived_ids))]
  transfers between devices with their start and end apart: 2 -> 0, of which waited for: 2 -> 0; matrix products, arithmetic and copies ran while one was open for 3% -> 0% of each run, Pallas kernels for 0% -> 0%
where the time goes in v1:
time: 115 us
  Pallas kernels  97 us (84%)
  local copies, waits for them, and re-layouts  13.1 us (11%)
  other arithmetic  3.93 us (3%)
    pallas_call x1, Pallas kernels, run_pairs(): pl.pallas_call(functools.partial(pair_kernel, per_dev), out_shape=(jax.Sh...  70.4 us
    pallas_call x1, Pallas kernels, gather_blocks(): pl.pallas_call(functools.partial(gather_kernel, libs, tmpls), out_shape=j...  18.5 us
    unnamed x12, local copies, waits for them, and re-layouts  9.48 us
    pallas_call x1, Pallas kernels, send_back(): pl.pallas_call(functools.partial(return_kernel, libs, tmpls), out_shape=(...  8.17 us

profile of v1, /device:TPU:0, one launch (start us, length us, event | category | flops | bytes accessed | tf_op | source)
XLA Modules:
  0.0 114.8 jit_solution(8780080653147569537)
XLA Ops:
  0.6 0.0 copy-start
  0.6 0.0 copy-start.1
  0.7 0.8 slice_bitcast_fusion.1
  1.5 0.9 select_reduce_fusion
  2.4 0.8 copy.32
  3.2 0.7 multiply_add_fusion
  3.9 0.1 copy.31
  4.0 0.7 convert_element_type.12
  4.7 1.5 %stack.23.own_ref = f32[32,8,128]{2,1,0:T(8,128)} concatenate(f32[32,3,128]{2,1,0:T(4,128)S(1)} %copy.32, f32[32,1,128]{2,1,0:T(1,128)S(1)} %bitcast.16, f32[32,1,128]{2,1,0:T(1,128)} %bitcast.19, f32[32,1,128]{2,1,0:T(1,128)S(1)} %bitcast.15, f32[32,1,128]{2,1,0:T(1,128)S(1)} %bitcast.18, f32[32,1,128]{2,1,0:T(1,128)S(1)} %bitcast.17), dimensions={1} | concatenate | bytes 262144 | tf_op jit(solution)/shard_map/stack | solution.py:310
  6.2 18.5 %shard_map.121 = f32[4,2,32,8,128]{4,3,2,1,0:T(8,128)} custom-call(f32[32,8,128]{2,1,0:T(8,128)} %stack.23.own_ref), custom_call_target="tpu_custom_call" | custom-call | tf_op jit(solution)/shard_map/pallas_call | solution.py:99
  24.7 1.4 %fusion = s32[8,32,1,4]{3,2,1,0:T(1,128)S(1)} fusion(f32[8,32,8,128]{3,2,1,0:T(8,128)} %bitcast.12, s32[]{:T(128)S(6)} %mul.15), kind=kLoop, calls=%fused_computation.4 | loop fusion | flops 2048 | bytes 8196 | tf_op jit(solution)/shard_map/sub | solution.py:314
  26.1 0.2 select_reduce_fusion.2
  26.4 0.6 reshape.19.slot_ref
  27.0 0.0 copy-done
  27.0 1.5 %copy.33.points_ref = f32[512,3,128]{2,1,0:T(4,128)} copy(f32[512,3,128]{2,0,1:T(8,128)S(1)} %copy-done) | data formatting | bytes 1572864 | tf_op args[8]
  28.5 0.0 copy-done.1
  28.5 0.0 copy-start.2
  28.5 1.5 %copy.34.weights_ref = bf16[512,5,128]{2,1,0:T(8,128)(2,1)} copy(bf16[512,5,128]{2,0,1:T(8,128)(2,1)S(1)} %copy-done.1) | data formatting | bytes 1310720 | tf_op args[9]
  30.0 70.4 %shard_map.122 = (f32[512,5,128]{2,1,0:T(8,128)}, f32[8,4,128]{2,1,0:T(4,128)}) custom-call(s32[256]{0:T(256)} %reshape.19.slot_ref, f32[5]{0:T(128)} %widths_ref.1, f32[8,32,8,128]{3,2,1,0:T(8,128)} %bitcast.13, f32[512,3,128]{2,1,0:T(4,128)} %copy.33.points_ref, bf16[512,5,128]{2,1,0:T(8,128)(2,1)} %copy.34.weights_ref), custom_call_target="tpu_custom_call" | custom-call | tf_op jit(solution)/shard_map/pallas_call | solution.py:223
  100.4 0.0 copy-done.2
  100.4 0.6 pad.9.owner_ref
  101.0 8.2 %shard_map.123 = (f32[32,4]{1,0:T(8,128)}, f32[32,12]{1,0:T(8,128)}) custom-call(f32[8,4,128]{2,1,0:T(4,128)} %get-tuple-element.7.res_ref, s32[8,128]{1,0:T(8,128)} %pad.9.owner_ref), custom_call_target="tpu_custom_call" | custom-call | tf_op jit(solution)/shard_map/pallas_call | solution.py:291
  109.1 1.4 %copy.36 = f32[32,12]{0,1:T(8,128)} copy(f32[32,12]{1,0:T(8,128)} %get-tuple-element.18) | data formatting | bytes 3072
  110.5 1.4 %copy.35 = f32[32,4]{0,1:T(4,128)} copy(f32[32,4]{1,0:T(8,128)} %get-tuple-element.17) | data formatting | bytes 1024
  111.9 2.9 %copy.37 = f32[512,5,128]{2,0,1:T(8,128)} copy(f32[512,5,128]{2,1,0:T(8,128)} %get-tuple-element.19) | data formatting | bytes 2621440
  (2 shorter events, 0.0 us)
Async XLA Ops:
  0.6 26.4 %copy-start = (f32[512,3,128]{2,0,1:T(8,128)S(1)}, f32[512,3,128]{2,0,1:T(8,128)}, u32[]{:S(2)}) copy-start(f32[512,3,128]{2,0,1:T(8,128)} %param.18) | copy-start | bytes 2359300
  0.6 27.9 %copy-start.1 = (bf16[512,5,128]{2,0,1:T(8,128)(2,1)S(1)}, bf16[512,5,128]{2,0,1:T(8,128)(2,1)}, u32[]{:S(2)}) copy-start(bf16[512,5,128]{2,0,1:T(8,128)(2,1)} %param.19) | copy-start | bytes 1966084
  28.5 71.9 %copy-start.2 = (s32[32,4]{0,1:T(4,128)S(1)}, s32[32,4]{0,1:T(4,128)}, u32[]{:S(2)}) copy-start(s32[32,4]{0,1:T(4,128)} %param.14) | copy-start | bytes 1540

commit v2 on v1

v2 whole, which is shorter than its diff:
```python
import functools
import math

import jax
import jax.numpy as jnp
from jax import lax
from jax.experimental import pallas as pl
from jax.experimental.pallas import tpu as pltpu
from jax.sharding import PartitionSpec as P

MESH = pl.DeviceIdType.MESH
F32 = jnp.float32
BF16 = jnp.bfloat16
GROUP = 8
FLIP = True
VALUES = 16


def gather_kernel(libs, tmpls, xyz_ref, charge_ref, type_ref, chan_ref, owner_ref, slot_ref, real_ref, whole_ref, name_ref,
                  local_sem, z_send, z_recv, x_send, x_recv, s_send, s_recv):
    l = lax.axis_index("lib")
    t = lax.axis_index("tmpl")
    s = lax.axis_index("sub")
    half = real_ref.shape[3] // 2
    moves = [(xyz_ref, real_ref.at[l, t, pl.ds(0, 3)]), (charge_ref, real_ref.at[l, t, 3]), (type_ref, whole_ref.at[l, t, 0]),
             (chan_ref, whole_ref.at[l, t, 1]), (owner_ref, name_ref.at[l, t, 0]), (slot_ref, name_ref.at[l, t, 1])]
    moves = [pltpu.make_async_copy(src, dst, local_sem.at[n]) for n, (src, dst) in enumerate(moves)]
    for move in moves:
        move.start()
    barrier = pltpu.get_barrier_semaphore()

    @pl.loop(1, libs)
    def _(k):
        pl.semaphore_signal(barrier, inc=1, device_id={"lib": lax.rem(l + k, libs)}, device_id_type=MESH)

    @pl.loop(1, tmpls)
    def _(k):
        pl.semaphore_signal(barrier, inc=1, device_id={"tmpl": lax.rem(t + k, tmpls)}, device_id_type=MESH)

    pl.semaphore_signal(barrier, inc=1, device_id={"sub": 1 - s}, device_id_type=MESH)
    for move in moves:
        move.wait()
    pl.semaphore_wait(barrier, libs + tmpls - 1)

    def chunk(k, m):
        at = (lax.rem(l - k + libs, libs), lax.rem(t - m + tmpls, tmpls))
        part = pl.ds(s * half, half)
        return real_ref.at[at + (slice(None), part)], whole_ref.at[at + (slice(None), part)], name_ref.at[at + (s,)]

    class Bundle:
        def __init__(self, refs, send, recv, device):
            self.copies = [pltpu.make_async_remote_copy(
                src_ref=ref, dst_ref=ref, send_sem=send(n), recv_sem=recv(n), device_id=device, device_id_type=MESH)
                for n, ref in enumerate(refs)]

        def start(self):
            for c in self.copies:
                c.start()

        def wait_recv(self):
            for c in self.copies:
                c.wait_recv()

        def wait_send(self):
            for c in self.copies:
                c.wait_send()

    def z_copy(k):
        return Bundle(chunk(0, 0), lambda n: z_send.at[k, n], lambda n: z_recv.at[k, n], {"lib": lax.rem(l + k, libs)})

    def x_copy(k, m):
        return Bundle(chunk(k, 0), lambda n: x_send.at[k, m, n], lambda n: x_recv.at[k, m, n], {"tmpl": lax.rem(t + m, tmpls)})

    def s_copy(k, m):
        return Bundle(chunk(k, m), lambda n: s_send.at[k, m, n], lambda n: s_recv.at[k, m, n], {"sub": 1 - s})

    @pl.loop(1, tmpls)
    def _(m):
        x_copy(0, m).start()

    @pl.loop(1, libs)
    def _(k):
        z_copy(k).start()

    @pl.loop(1, libs)
    def _(k):
        z_copy(k).wait_recv()

        @pl.loop(1, tmpls)
        def _(m):
            x_copy(k, m).start()

        s_copy(k, 0).start()

    @pl.loop(1, tmpls)
    def _(m):
        @pl.loop(0, libs)
        def _(k):
            x_copy(k, m).wait_recv()
            s_copy(k, m).start()

    @pl.loop(1, libs)
    def _(k):
        z_copy(k).wait_send()
        s_copy(k, 0).wait_send()
        s_copy(k, 0).wait_recv()

    @pl.loop(1, tmpls)
    def _(m):
        @pl.loop(0, libs)
        def _(k):
            x_copy(k, m).wait_send()
            s_copy(k, m).wait_send()
            s_copy(k, m).wait_recv()


def gather_blocks(xyz, charge, types, chans, owners, slots, libs, tmpls):
    dma = pltpu.SemaphoreType.DMA
    blocks = charge.shape[0]
    lead = (libs, tmpls)
    vmem = pl.BlockSpec(memory_space=pltpu.VMEM)
    return pl.pallas_call(
        functools.partial(gather_kernel, libs, tmpls),
        out_shape=(jax.ShapeDtypeStruct(lead + (4, blocks, 128), F32), jax.ShapeDtypeStruct(lead + (2, blocks, 128), jnp.int32),
                   jax.ShapeDtypeStruct(lead + (2,) + owners.shape, jnp.int32)),
        in_specs=[pl.BlockSpec(memory_space=pl.ANY)] * 6,
        out_specs=(vmem,) * 3,
        scratch_shapes=[dma((6,)), dma((libs, 3)), dma((libs, 3)), dma(lead + (3,)), dma(lead + (3,)),
                        dma(lead + (3,)), dma(lead + (3,))],
        compiler_params=pltpu.CompilerParams(collective_id=0, has_side_effects=True, vmem_limit_bytes=60 << 20),
    )(xyz, charge, types, chans, owners, slots)


def split3(a):
    h = a.astype(BF16).astype(F32)
    r = a - h
    m = r.astype(BF16).astype(F32)
    return h, m, r - m


def split2(a):
    h = a.astype(BF16)
    return h, (a - h.astype(F32)).astype(BF16)


def pair_kernel(slot_ref, widths_ref, table_ref, real_ref, whole_ref, points_ref, bf_weights_ref, wg_ref, out_ref, res_ref,
                atom_ref, weights_ref):
    devices, _, per_dev, _ = real_ref.shape
    res_ref[...] = jnp.zeros_like(res_ref)
    row = lax.broadcasted_iota(jnp.int32, (8, 128), 0)
    row16 = lax.broadcasted_iota(jnp.int32, (VALUES, 128), 0)
    lane16 = lax.broadcasted_iota(jnp.int32, (VALUES, 128), 1)
    low = row < 4
    log2e = math.log2(math.e)
    wide = [widths_ref[f] for f in range(5)]
    scale = [-log2e * w for w in wide]

    @pl.loop(0, 5)
    def _(f):
        wg_ref[f] = jnp.zeros(wg_ref.shape[1:], F32)
        weights_ref[f] = bf_weights_ref[f].astype(F32)

    @pl.loop(0, devices)
    def _(dev):
        types = whole_ref[dev, 0]
        chan = whole_ref[dev, 1]
        steric = jnp.zeros(types.shape, F32)
        strength = jnp.zeros(types.shape, F32)
        for n in range(table_ref.shape[0]):
            same = types == n
            steric = jnp.where(same, table_ref[n, 0], steric)
            strength = jnp.where(same, table_ref[n, 1], strength)
        atom_ref[dev, 0] = steric
        atom_ref[dev, 1] = strength
        atom_ref[dev, 2] = jnp.where(chan == 0, scale[2], jnp.where(chan == 1, scale[3], scale[4]))

    def one(dev, b, slot):
        valid = jnp.where(slot >= 0, F32(1), F32(0))
        slot = jnp.maximum(slot, 0)
        here = pl.ds(b, 1)
        there = pl.ds(slot, 1)
        x = [jnp.broadcast_to(real_ref[dev, c, here, :], (8, 128)) for c in range(3)]
        y = [jnp.broadcast_to(points_ref[c, there, :], (8, 128)) for c in range(3)]
        chan = whole_ref[dev, 1, here, :]
        steric = atom_ref[dev, 0, here, :] * valid
        charge = real_ref[dev, 3, here, :] * valid
        strength = atom_ref[dev, 1, here, :] * valid
        pharm_scale = atom_ref[dev, 2, here, :]

        def rows(first, norm_row, one_row, p):
            norm = p[0] * p[0] + p[1] * p[1] + p[2] * p[2]
            v = jnp.where(row == 0, p[0] * first, jnp.where(row == 1, p[1] * first, p[2] * first))
            return jnp.where(row < 3, v, jnp.where(row == norm_row, norm, jnp.where(row == one_row, 1.0, 0.0)))

        def atom_side(v):
            h, m, l = split3(v)
            return jnp.concatenate([h, h, h, m, m, l], axis=0).astype(BF16)

        xv = rows(1.0, 3, 4, x)
        xs = atom_side(xv)
        yh, ym, yl = split3(rows(-2.0, 4, 3, y))
        ys = jnp.concatenate([yh, ym, yl, yh, ym, yh], axis=0).astype(BF16)
        if FLIP:
            both = jnp.concatenate([xs, atom_side(xv * pharm_scale)], axis=1)
            dist = lax.dot_general(both, ys, (((0,), (0,)), ((), ())), preferred_element_type=F32)
            dist, pharm = dist[:128], dist[128:]
        else:
            dist = lax.dot_general(ys, xs, (((0,), (0,)), ((), ())), preferred_element_type=F32)
            pharm = dist * pharm_scale
        inner = jnp.where(row % 4 == 0, 1.0, jnp.where(row % 4 == 1, x[0], jnp.where(row % 4 == 2, x[1], x[2])))
        outer = jnp.concatenate([jnp.where(low, 1.0, x[0]), jnp.where(low, x[1], x[2])], axis=0)
        moments = outer * jnp.concatenate([inner, inner], axis=0)

        def contract(exps, coefs):
            hi, lo = split2(exps)
            rhs = jnp.concatenate([hi, lo], axis=0 if FLIP else 1)
            lhs = jnp.concatenate([moments * c for c in coefs], axis=0)
            lh, ll = split2(lhs)
            lhs2 = jnp.concatenate([lh, ll], axis=0)
            lhs2 = jnp.concatenate([lhs2, lhs2], axis=1)
            got = lax.dot_general(lhs2, rhs, (((1,), (0 if FLIP else 1,)), ((), ())), preferred_element_type=F32)
            n = VALUES * len(coefs)
            got = got[:n] + got[n:]
            return [got[VALUES * c:VALUES * (c + 1)] for c in range(len(coefs))]

        parts = contract(jnp.exp2(dist * scale[0]), [steric]) + contract(jnp.exp2(dist * scale[1]), [charge])
        parts += contract(jnp.exp2(pharm), [jnp.where(chan == c, strength, 0.0) for c in range(3)])
        total = jnp.zeros((VALUES, 128), F32)
        score = jnp.zeros((1, 128), F32)
        for f in range(5):
            v = weights_ref[f, there, :]
            score = score + v * parts[f][0:1]
            total = total + (v * (-2.0 * wide[f])) * parts[f]
        base = jnp.concatenate([total[0:4]] * 4, axis=0)
        y16 = jnp.concatenate([jnp.where(low, 0.0, y[0]), jnp.where(low, y[1], y[2])], axis=0)
        final = jnp.where(row16 == 0, score, total - y16 * base)
        summed = jnp.sum(final, axis=1, keepdims=True)
        return there, [p[0:1] for p in parts], summed

    group = math.gcd(GROUP, per_dev)

    @pl.loop(0, devices)
    def _(dev):
        @pl.loop(0, per_dev // group)
        def _(g):
            slots = [slot_ref[dev, g * group + u] for u in range(group)]
            best = slots[0]
            for v in slots[1:]:
                best = jnp.maximum(best, v)

            @pl.when(best >= 0)
            def _():
                done = [one(dev, g * group + u, slots[u]) for u in range(group)]
                for there, wparts, summed in done:
                    for f, part in enumerate(wparts):
                        wg_ref[f, there, :] += part
                acc = res_ref[dev]
                for u, (there, wparts, summed) in enumerate(done):
                    acc = jnp.where(lane16 == g * group + u, summed, acc)
                res_ref[dev] = acc

    @pl.loop(0, devices)
    def _(dev):
        r = res_ref[dev]
        packed = r[0:4]
        for q in range(1, 4):
            packed = packed + pltpu.roll(r[4 * q:4 * q + 4], 32 * q, 1)
        out_ref[dev] = packed


def run_pairs(slots, widths, table, real, whole, points, weights):
    tmpl_count = points.shape[1]
    devices, _, per_dev, _ = real.shape
    vmem = pl.BlockSpec(memory_space=pltpu.VMEM)
    smem = pl.BlockSpec(memory_space=pltpu.SMEM)
    return pl.pallas_call(
        pair_kernel,
        out_shape=(jax.ShapeDtypeStruct((5, tmpl_count, 128), F32), jax.ShapeDtypeStruct((devices, 4, 128), F32)),
        in_specs=[smem, smem, smem, vmem, vmem, vmem, vmem],
        out_specs=(vmem, vmem),
        scratch_shapes=[pltpu.VMEM((devices, VALUES, 128), F32), pltpu.VMEM((devices, 3, per_dev, 128), F32),
                        pltpu.VMEM((5, tmpl_count, 128), F32)],
        compiler_params=pltpu.CompilerParams(vmem_limit_bytes=60 << 20),
    )(slots, widths, table, real, whole, points, weights)


def return_kernel(libs, tmpls, res_ref, owner_ref, score_ref, pose_ref, got_ref, local_sem, send_sem, recv_sem):
    l = lax.axis_index("lib")
    t = lax.axis_index("tmpl")
    s = lax.axis_index("sub")
    owners = libs * tmpls
    count = 2 * owners
    me = (l * tmpls + t) * 2 + s
    barrier = pltpu.get_barrier_semaphore()

    def peer(k):
        other = lax.rem(me + k, count)
        return other // 2, {"lib": other // (2 * tmpls), "tmpl": lax.rem(other // 2, tmpls), "sub": lax.rem(other, 2)}

    @pl.loop(1, count)
    def _(k):
        pl.semaphore_signal(barrier, inc=1, device_id=peer(k)[1], device_id_type=MESH)

    local = pltpu.make_async_copy(res_ref.at[l * tmpls + t], got_ref.at[me], local_sem)
    local.start()
    pl.semaphore_wait(barrier, count - 1)

    def copy(k):
        block, where = peer(k)
        return pltpu.make_async_remote_copy(
            src_ref=res_ref.at[block], dst_ref=got_ref.at[me], send_sem=send_sem.at[k], recv_sem=recv_sem.at[k],
            device_id=where, device_id_type=MESH)

    @pl.loop(1, count)
    def _(k):
        copy(k).start()

    local.wait()

    @pl.loop(1, count)
    def _(k):
        copy(k).wait()

    owner = owner_ref[...]
    per_block, blocks = owner.shape

    def add(o, carry):
        total, scores = carry
        both = got_ref[2 * o] + got_ref[2 * o + 1]
        scores = jnp.where(owner == o, jnp.broadcast_to(both[0:1, :blocks], (per_block, blocks)), scores)
        return total + both, scores

    total, scores = lax.fori_loop(0, owners, add, (jnp.zeros((4, 128), F32), jnp.zeros((per_block, blocks), F32)))
    rows = [total] + [pltpu.roll(total, 128 - 32 * q, 1) for q in range(1, 4)]
    pose = jnp.concatenate([rows[1][0:1], rows[2][0:1], rows[3][0:1], rows[1][1:4], rows[2][1:4], rows[3][1:4]], axis=0)
    score_ref[...] = scores
    pose_ref[...] = pose[:, :blocks]


def send_back(res, owner_rows, libs, tmpls):
    per_block, blocks = owner_rows.shape
    dma = pltpu.SemaphoreType.DMA
    count = 2 * libs * tmpls
    vmem = pl.BlockSpec(memory_space=pltpu.VMEM)
    return pl.pallas_call(
        functools.partial(return_kernel, libs, tmpls),
        out_shape=(jax.ShapeDtypeStruct((per_block, blocks), F32), jax.ShapeDtypeStruct((12, blocks), F32)),
        in_specs=[vmem, vmem],
        out_specs=(vmem, vmem),
        scratch_shapes=[pltpu.VMEM((count, 4, 128), F32), dma, dma((count,)), dma((count,))],
        compiler_params=pltpu.CompilerParams(collective_id=1, has_side_effects=True),
    )(res, owner_rows)


def local(libs, tmpls, coords, atom_type, channel, charge, pair_owner, pair_slot, type_table, widths, tmpl_points,
          tmpl_weights):
    owners, slots = pair_owner.T, pair_slot.T
    real, whole, names = gather_blocks(jnp.transpose(coords, (1, 0, 2)), charge, atom_type, channel, owners, slots, libs, tmpls)
    count = libs * tmpls
    real, whole, names = [a.reshape((count,) + a.shape[2:]) for a in (real, whole, names)]
    me = lax.axis_index("lib") * tmpls + lax.axis_index("tmpl")
    chosen = jnp.max(jnp.where(names[:, 0] == me, names[:, 1], -1), axis=1)
    weight_grad, res = run_pairs(chosen, widths, type_table, real, whole, jnp.transpose(tmpl_points, (1, 0, 2)),
                                 jnp.transpose(tmpl_weights, (1, 0, 2)))
    scores, pose = send_back(res, owners, libs, tmpls)
    return scores.T, pose.T, jnp.transpose(weight_grad, (1, 0, 2))


def solution(mesh):
    every = ("groups", "lib", "tmpl")
    in_specs = (P(every, None, None), P(every, None), P(every, None), P(every, None), P(every, None), P(every, None),
                P(), P(), P(("lib", "tmpl"), None, "sub"), P(("lib", "tmpl"), None, "sub"))
    out_specs = (P(every, None), P(every, None), P(every, None, "sub"))
    body = functools.partial(local, mesh.shape["lib"], mesh.shape["tmpl"])
    return jax.shard_map(body, mesh=mesh, in_specs=in_specs, out_specs=out_specs, check_vma=False)
```

time: 115 us -> 89.7 us (0.78)
  Pallas kernels: 97 us -> 83.7 us
  local copies, waits for them, and re-layouts: 13.1 us -> 3.88 us
  other arithmetic: 3.93 us -> 1.34 us
    pallas_call x2, Pallas kernels: 88.9 us -> 74.1 us  [the longest x1 57.2 us: run_pairs(): pl.pallas_call(pair_kernel, out_shape=(jax.ShapeDtypeStruct((5, tmpl_coun...]
    unnamed x12 -> x3, local copies, waits for them, and re-layouts: 9.48 us -> 3.88 us
    another operation x1 -> x0, local copies, waits for them, and re-layouts: 1.51 us -> none  [local(): jnp.stack([coords[:, 0], coords[:, 1], coords[:, 2], steric, charge, stre...]
    pallas_call x1, Pallas kernels: 8.17 us -> 9.63 us  [send_back(): pl.pallas_call(functools.partial(return_kernel, libs, tmpls), out_shape=(...]
    sub x1 -> x0, other arithmetic: 1.4 us -> none  [local(): ids = gathered[:, :, 7, :per_block].astype(jnp.int32) - me * tmpl_count]
where the time goes in v2:
time: 89.7 us; the launch traced here: 89.6 us
  Pallas kernels  83.7 us (93%)
  local copies, waits for them, and re-layouts  3.88 us (4%)
  other arithmetic  1.34 us (1%)
    pallas_call x1, Pallas kernels, run_pairs(): pl.pallas_call(pair_kernel, out_shape=(jax.ShapeDtypeStruct((5, tmpl_coun...  57.2 us
    pallas_call x1, Pallas kernels, gather_blocks(): pl.pallas_call(functools.partial(gather_kernel, libs, tmpls), out_shape=(...  16.9 us
    pallas_call x1, Pallas kernels, send_back(): pl.pallas_call(functools.partial(return_kernel, libs, tmpls), out_shape=(...  9.63 us
    unnamed x3, local copies, waits for them, and re-layouts  3.88 us

profile of v2, /device:TPU:0, one launch (start us, length us, event | category | flops | bytes accessed | tf_op | source)
XLA Modules:
  0.0 89.6 jit_solution(14074834413785400411)
XLA Ops:
  0.6 1.4 %copy.13.table_ref = f32[16,2]{1,0:T(8,128)} copy(f32[16,2]{0,1:T(2,128)} %param.16) | data formatting | bytes 256 | tf_op args[6]
  2.0 16.9 %shard_map.121 = (f32[4,2,4,32,128]{4,3,2,1,0:T(8,128)}, s32[4,2,2,32,128]{4,3,2,1,0:T(8,128)}, s32[4,2,2,4,32]{4,3,2,1,0:T(4,128)}) custom-call(f32[3,32,128]{2,1,0:T(8,128)} %bitcast.15, f32[32,128]{1,0:T(8,128)} %charge_ref.1, s32[32,128]{1,0:T(8,128)} %type_ref.1, s32[32,128]{1,0:T(8,128)} %chan_ref.1, s32[4,32]{1,0:T(4,128)} %bitcast.17, s32[4,32]{1,0:T(4,128)} %bitcast.20), custom_call_target="tpu_custom_call" | custom-call | tf_op jit(solution)/shard_map/pallas_call | solution.py:122
  18.9 1.3 %fusion.slot_ref = s32[8,32]{1,0:T(8,128)} fusion(s32[8,2,4,32]{3,2,1,0:T(4,128)} %bitcast.16, s32[]{:T(128)S(6)} %add.3), kind=kLoop, calls=%fused_computation.1 | loop fusion | flops 2816 | bytes 9220 | tf_op jit(solution)/shard_map/reduce_max | solution.py:362
  20.2 57.2 %shard_map.122 = (f32[5,512,128]{2,1,0:T(8,128)}, f32[8,4,128]{2,1,0:T(4,128)}) custom-call(s32[8,32]{1,0:T(8,128)} %fusion.slot_ref, f32[5]{0:T(128)} %widths_ref.1, f32[16,2]{1,0:T(8,128)} %copy.13.table_ref, f32[8,4,32,128]{3,2,1,0:T(8,128)} %bitcast.13, s32[8,2,32,128]{3,2,1,0:T(8,128)} %bitcast.14, f32[3,512,128]{2,1,0:T(8,128)} %bitcast.11, ...), custom_call_target="tpu_custom_call" | custom-call | tf_op jit(solution)/shard_map/pallas_call | solution.py:276
  77.5 9.6 %shard_map.123 = (f32[4,32]{1,0:T(4,128)}, f32[12,32]{1,0:T(8,128)}) custom-call(f32[8,4,128]{2,1,0:T(4,128)} %get-tuple-element.13.res_ref, s32[4,32]{1,0:T(4,128)} %bitcast.18), custom_call_target="tpu_custom_call" | custom-call | tf_op jit(solution)/shard_map/pallas_call | solution.py:345
  87.1 1.2 %copy.16 = f32[32,4]{0,1:T(4,128)} copy(f32[32,4]{0,1:T(4,128)} %bitcast.21) | data formatting | bytes 1024
  88.3 1.3 %copy.17 = f32[32,12]{0,1:T(8,128)} copy(f32[32,12]{0,1:T(8,128)} %bitcast.19) | data formatting | bytes 3072
